TPU v7x, 32 devices: a whole 2x2x4 slice. The times are simulated.
32 devices in a mesh: clip: 4 (over z), sp: 4 (over x, core), tp: 2 (over y).
Axes of the slice: x: 2, y: 2, z: 4, core: 2. Of those that a mesh axis runs over, the one named last changes fastest.
Arguments:
- latents: bfloat16 [4, 4, 1024, 512], P('clip', 'sp', None, 'tp'), may hold values from -6 to 6
- saved_input: bfloat16 [4, 4, 1024, 512], P('clip', None, 'sp', 'tp'), may hold values from -6 to 6
- out_grad: bfloat16 [4, 4, 1024, 512], P('clip', None, 'sp', 'tp'), may hold values from -6 to 6
- temporal_weight: bfloat16 [3, 512, 512], P(None, 'tp'), may hold values from -0.15625 to 0.15625
- spatial_weight: bfloat16 [9, 512, 512], P(None, 'tp'), may hold values from -0.09375 to 0.09375
Outputs:
- input_grad: bfloat16 [4, 4, 1024, 512], P('clip', 'sp', None, 'tp')
- temporal_grad: float32 [3, 512, 512], P(None, 'tp', 'sp')
- spatial_grad: float32 [9, 512, 512], P(None, 'tp', 'sp')
All inputs are finite; a program needn't handle non-finite values.
Results may differ from a plain program's by a relative error of at most 0.005.
Values may be sent and summed in bfloat16 or wider, within the bound.
A program may use at most 64 MiB of HBM per device.

v0:
```python
import math

import jax
import jax.numpy as jnp
from jax import lax
from jax.sharding import PartitionSpec as P

HS = 32
WS = 32


def pad_frames(values):
    return jnp.pad(values, ((0, 0), (1, 1), (0, 0), (0, 0)))


def local(latents, saved_input, out_grad, temporal_weight, spatial_weight):
    clips_all = latents.shape[0] * lax.axis_size("clip")
    frames_all = latents.shape[1] * lax.axis_size("sp")
    scale_factor = 1.0 / math.sqrt(clips_all * frames_all * HS * WS)
    frames_count = out_grad.shape[1]
    local_in = temporal_weight.shape[1]
    saved_padded = pad_frames(saved_input)
    block_in = lax.all_gather(out_grad, "tp", axis=3, tiled=True)
    columns = temporal_weight
    padded = pad_frames(block_in)
    hidden_acc = jnp.zeros(out_grad.shape[:3] + (local_in,), jnp.float32)
    parts = []
    for tap_index in range(3):
        shifted = padded[:, 2 - tap_index : 2 - tap_index + frames_count]
        hidden_acc = hidden_acc + jnp.einsum(
            "bfpo,io->bfpi", shifted, columns[tap_index], preferred_element_type=jnp.float32
        )
        parts.append(
            jnp.einsum(
                "bfpi,bfpo->io",
                saved_padded[:, tap_index : tap_index + frames_count],
                block_in,
                preferred_element_type=jnp.float32,
            )
        )
    weight_acc = jnp.stack(parts)
    hidden_acc, temporal_local = (hidden_acc, weight_acc)
    hidden_grad = hidden_acc.astype(jnp.bfloat16)
    regrouped = lax.all_to_all(hidden_grad, "sp", split_axis=1, concat_axis=2, tiled=True)
    batch = latents.shape[0] * latents.shape[1]
    image_pad = jnp.pad(latents.reshape(batch, HS, WS, local_in), ((0, 0), (1, 1), (1, 1), (0, 0)))
    block_in = lax.all_gather(regrouped, "tp", axis=3, tiled=True)
    widths = block_in.shape[3]
    columns = spatial_weight
    plain = block_in.reshape(batch, HS, WS, widths)
    grid = jnp.pad(plain, ((0, 0), (1, 1), (1, 1), (0, 0)))
    input_acc = jnp.zeros((batch, HS, WS, local_in), jnp.float32)
    parts = []
    for row_shift in (-1, 0, 1):
        for col_shift in (-1, 0, 1):
            tap_index = 3 * (row_shift + 1) + (col_shift + 1)
            moved = grid[:, 1 - row_shift : 1 - row_shift + HS, 1 - col_shift : 1 - col_shift + WS]
            input_acc = input_acc + jnp.einsum(
                "gabo,co->gabc", moved, columns[tap_index], preferred_element_type=jnp.float32
            )
            window = image_pad[
                :, 1 + row_shift : 1 + row_shift + HS, 1 + col_shift : 1 + col_shift + WS
            ]
            parts.append(
                jnp.einsum("gabc,gabo->co", window, plain, preferred_element_type=jnp.float32)
            )
    weight_acc = jnp.stack(parts)
    input_acc, spatial_local = (input_acc, weight_acc)
    input_grad = input_acc.reshape(latents.shape).astype(jnp.bfloat16)
    temporal_scaled = temporal_local * scale_factor
    spatial_scaled = spatial_local * scale_factor
    spread = (
        lax.psum_scatter(temporal_scaled, "sp", scatter_dimension=2, tiled=True),
        lax.psum_scatter(spatial_scaled, "sp", scatter_dimension=2, tiled=True),
    )
    temporal_grad, spatial_grad = lax.psum((spread[0], spread[1]), "clip")
    return (input_grad, temporal_grad, spatial_grad)


def solution(mesh):
    return jax.shard_map(
        local,
        mesh=mesh,
        in_specs=(
            P("clip", "sp", None, "tp"),
            P("clip", None, "sp", "tp"),
            P("clip", None, "sp", "tp"),
            P(None, "tp", None),
            P(None, "tp", None),
        ),
        out_specs=(P("clip", "sp", None, "tp"), P(None, "tp", "sp"), P(None, "tp", "sp")),
        check_vma=False,
    )
```

profile of v0, /device:TPU:0, one launch (start us, length us, event | category | flops | bytes accessed | tf_op | source)
XLA Modules:
  0.0 231.4 jit_solution(14981217738277615913)
XLA Ops:
  7.2 0.0 copy-start.4
  7.2 0.0 all-gather.3.cloned.1.call-start
  7.2 0.7 all-gather.3.cloned.1.call-update
  7.9 0.0 all-gather.5.cloned.1.call-start
  8.0 25.6 %all-gather.3.cloned.1.call-done = bf16[1,4,256,512]{3,2,1,0:T(8,128)(2,1)} async-done(((bf16[1,4,256,256]{3,2,1,0:T(8,128)(2,1)}), bf16[1,4,256,512]{3,2,1,0:T(8,128)(2,1)}) %all-gather.3.cloned.1.call-update) | async-done | bytes 1048592 | tf_op jit(solution)/shard_map/all_gather | solution.py:23
  33.5 0.0 copy-start.1
  33.5 1.7 fusion.30
  35.3 0.0 copy-done.4
  35.3 0.0 copy-done.1
  35.3 0.5 convolution_add_fusion.9
  35.8 0.0 copy-start.3
  35.8 0.5 fusion.2
  36.2 11.9 %all_to_all.12 = bf16[1,4,256,256]{3,2,0,1:T(8,128)(2,1)} all-to-all(bf16[1,4,256,256]{3,2,0,1:T(8,128)(2,1)S(1)} %fusion.2), channel_id=1, replica_groups=mesh['clip'=4,'sp'=4,'tp'=2] {'sp'}, dimensions={1} | all-to-all | bytes 1048576 | tf_op jit(solution)/shard_map/all_to_all | solution.py:44
  48.1 0.0 all-gather.5.cloned.1.call-update
  48.2 0.0 reduce-scatter.3.cloned.1.call-start
  48.2 0.0 copy-done.3
  48.2 0.2 copy.12
  48.4 0.4 convolution_bitcast_fusion.1
  48.9 0.4 convolution_bitcast_fusion.3
  49.3 0.5 convolution_bitcast_fusion.2
  49.8 0.0 copy-start.5
  49.8 1.3 maximum_multiply_fusion
  51.1 0.0 reduce-scatter.3.cloned.1.call-update
  51.2 0.0 reduce-scatter.5.cloned.1.call-start
  51.2 17.5 %all-gather.5.cloned.1.call-done = bf16[1,1,1024,512]{3,2,1,0:T(8,128)(2,1)} async-done(((bf16[1,1,1024,256]{3,2,1,0:T(8,128)(2,1)}), bf16[1,1,1024,512]{3,2,1,0:T(8,128)(2,1)}) %all-gather.5.cloned.1.call-update) | async-done | bytes 1048592 | tf_op jit(solution)/shard_map/all_gather | solution.py:47
  68.7 0.0 copy-done.5
  68.7 0.0 copy-start
  68.7 1.8 fusion.11
  70.5 0.0 copy-done
  70.5 0.5 fusion.10
  70.9 0.5 fusion.9
  71.4 0.5 fusion.8
  71.9 0.5 fusion.3
  72.4 0.5 fusion.7
  72.9 0.5 fusion.6
  73.3 0.5 fusion.5
  73.8 0.5 fusion.4
  74.3 2.9 %broadcast_multiply_fusion = f32[9,256,512]{2,1,0:T(8,128)} fusion(f32[9,256,512]{2,1,0:T(8,128)S(1)} %fusion.4), kind=kLoop, calls=%fused_computation | loop fusion | flops 1179648 | bytes 9437184 | tf_op jit(solution)/shard_map/mul | solution.py:71
  77.2 0.0 reduce-scatter.5.cloned.1.call-update
  77.2 0.0 all-reduce.7.cloned.1.call-start
  77.3 1.4 fusion.13
  78.7 1.4 convolution_add_fusion.7
  80.1 1.4 convolution_add_fusion.6
  81.6 17.6 %reduce-scatter.3.cloned.1.call-done = f32[3,256,128]{2,1,0:T(8,128)} async-done(((f32[3,256,512]{2,1,0:T(8,128)}), f32[3,256,128]{2,1,0:T(8,128)}) %reduce-scatter.3.cloned.1.call-update) | async-done | bytes 393232 | tf_op jit(solution)/shard_map/reduce_scatter | solution.py:73
  99.2 50.3 %reduce-scatter.5.cloned.1.call-done = f32[9,256,128]{2,1,0:T(8,128)} async-done(((f32[9,256,512]{2,1,0:T(8,128)}), f32[9,256,128]{2,1,0:T(8,128)}) %reduce-scatter.5.cloned.1.call-update) | async-done | bytes 1179664 | tf_op jit(solution)/shard_map/reduce_scatter | solution.py:74
  149.5 0.0 all-reduce.7.cloned.1.call-update
  149.5 0.0 copy-start.2
  149.5 1.6 convolution_add_fusion.5
  151.1 0.1 copy-done.2
  151.3 0.5 convolution_add_fusion.4
  151.7 0.5 convolution_add_fusion.3
  152.2 0.5 convolution_add_fusion.2
  152.7 0.5 convolution_add_fusion.1
  153.2 1.3 fusion.1
  154.5 66.3 %all-reduce.7.cloned.1.call-done = (f32[3,256,128]{2,1,0:T(8,128)}, f32[9,256,128]{2,1,0:T(8,128)}) async-done(((f32[3,256,128]{2,1,0:T(8,128)}, f32[9,256,128]{2,1,0:T(8,128)}), (f32[3,256,128]{2,1,0:T(8,128)}, f32[9,256,128]{2,1,0:T(8,128)})) %all-reduce.7.cloned.1.call-update) | async-done | bytes 1572880 | tf_op jit(solution)/shard_map/psum | solution.py:76
  220.8 1.8 copy.27
  222.5 2.4 %copy.28 = f32[9,256,128]{2,1,0:T(8,128)} copy(f32[9,256,128]{2,1,0:T(8,128)} %get-tuple-element.7) | data formatting | bytes 2359296
Async XLA Ops:
  7.2 28.1 %copy-start.4 = (bf16[3,256,512]{2,1,0:T(8,128)(2,1)S(1)}, bf16[3,256,512]{2,1,0:T(8,128)(2,1)}, u32[]{:S(2)}) copy-start(bf16[3,256,512]{2,1,0:T(8,128)(2,1)} %param.8) | copy-start | bytes 2359300
  7.2 26.4 %all-gather.3.cloned.1.call-start = ((), (), s32[]{:S(2)}) async-start(), calls=%async_computation.3 | async-start | bytes 1572864 | tf_op jit(solution)/shard_map/all_gather | solution.py:23
  7.9 60.8 %all-gather.5.cloned.1.call-start = ((), (), s32[]{:S(2)}) async-start(), calls=%async_computation.4 | async-start | bytes 1572864 | tf_op jit(solution)/shard_map/all_gather | solution.py:47
  33.5 1.8 copy-start.1
  35.8 12.5 %copy-start.3 = (bf16[1,4,256,256]{3,2,1,0:T(8,128)(2,1)S(1)}, bf16[1,4,256,256]{3,2,1,0:T(8,128)(2,1)}, u32[]{:S(2)}) copy-start(bf16[1,4,256,256]{3,2,1,0:T(8,128)(2,1)} %param.6) | copy-start | bytes 1572868
  48.2 51.1 %reduce-scatter.3.cloned.1.call-start = ((), (), s32[]{:S(2)}) async-start(), calls=%async_computation.5 | async-start | bytes 1966080 | tf_op jit(solution)/shard_map/reduce_scatter | solution.py:73
  49.8 18.9 %copy-start.5 = (bf16[1,1,1024,256]{3,2,1,0:T(8,128)(2,1)S(1)}, bf16[1,1,1024,256]{3,2,1,0:T(8,128)(2,1)}, u32[]{:S(2)}) copy-start(bf16[1,1,1024,256]{3,2,1,0:T(8,128)(2,1)} %param.5) | copy-start | bytes 1572868
  51.2 98.3 %reduce-scatter.5.cloned.1.call-start = ((), (), s32[]{:S(2)}) async-start(), calls=%async_computation.6 | async-start | bytes 5898240 | tf_op jit(solution)/shard_map/reduce_scatter | solution.py:74
  68.7 1.8 copy-start
  77.2 143.6 %all-reduce.7.cloned.1.call-start = ((), (), s32[]{:S(2)}) async-start(), calls=%async_computation.7 | async-start | bytes 3145728 | tf_op jit(solution)/shard_map/psum | solution.py:76
  149.5 1.7 copy-start.2
Sparse Core Ops, SparseCore 0:
  9.5 23.9 all-gather.2
  48.3 20.3 all-gather.4
  71.2 27.9 reduce-scatter.2
  101.6 47.8 reduce-scatter.4
  151.8 68.9 all-reduce.6
where the time goes:
time: 232 us; the launch traced here: 231 us
  waiting for transfers between devices  178 us (77%)
  matrix products  18.6 us (8%)
  between operations  14 us (6%)
  blocking collectives  11.9 us (5%)
  local copies, waits for them, and re-layouts  4.51 us (2%)
  other arithmetic  4.25 us (2%)
    psum x1, waiting for transfers between devices, local(): temporal_grad, spatial_grad = lax.psum((spread[0], spread[1]), 'clip')  66.3 us
    reduce_scatter x1, waiting for transfers between devices, local(): lax.psum_scatter(spatial_scaled, 'sp', scatter_dimension=2, tiled=True)  50.3 us
    all_gather x1, waiting for transfers between devices, local(): block_in = lax.all_gather(out_grad, 'tp', axis=3, tiled=True)  25.6 us
    reduce_scatter x1, waiting for transfers between devices, local(): lax.psum_scatter(temporal_scaled, 'sp', scatter_dimension=2, tiled=True)  17.6 us
    all_gather x1, waiting for transfers between devices, local(): block_in = lax.all_gather(regrouped, 'tp', axis=3, tiled=True)  17.5 us
    all_to_all x1, blocking collectives, local(): lax.all_to_all(hidden_grad, 'sp', split_axis=1, concat_axis=2, tiled=True)  11.9 us
    dot_general x9, matrix products, local(): jnp.einsum('gabo,co->gabc', moved, columns[tap_index], preferred_element_...  9.08 us
    dot_general x9, matrix products, local(): jnp.einsum('gabc,gabo->co', window, plain, preferred_element_type=jnp.flo...  5.52 us
  transfers between devices with their start and end apart: 5, of which 5 were waited for; matrix products, arithmetic and copies ran while one was open for 9% of the time, Pallas kernels for 0%

commit v1 on v0

v1 whole, which is shorter than its diff:
```python
import functools
import math

import jax
import jax.numpy as jnp
from jax import lax
from jax.experimental import pallas as pl
from jax.experimental.pallas import tpu as pltpu
from jax.sharding import PartitionSpec as P

HS = 32
WS = 32
MESH = pl.DeviceIdType.MESH
F32 = jnp.float32
BF16 = jnp.bfloat16


def pad_frames(values):
    return jnp.pad(values, ((0, 0), (1, 1), (0, 0), (0, 0)))


def nt(a, b):
    return lax.dot_general(a, b, (((1,), (1,)), ((), ())), preferred_element_type=F32)


def nn(a, b):
    return lax.dot_general(a, b, (((1,), (0,)), ((), ())), preferred_element_type=F32)


def chunks_of(taps, size):
    return [(start, min(size, taps - start)) for start in range(0, taps, size)]


def kernel(
    dims, lat, sav, og, tw, sw, ig, tg, sg,
    latv, savv, twv, swv, opad, hsend, hrecv, hwide, hs, savt, latt, acc,
    gsend, g1, g2s, g2r, gz, g3r, gq, gf,
    lsem, osend, orecv, osem, hsendsem, hrecvsem, hlocsem,
    s1s, s1r, s2s, s2r, s3s, s3r, s4s, s4r,
):
    S, T, Z, F, Pl, Cl, Cs, scale, chunks, KT = dims
    U = S // 2
    Q = Cl // Z
    HW = S * Pl
    C = T * Cl
    me_s, me_t, me_z = lax.axis_index("sp"), lax.axis_index("tp"), lax.axis_index("clip")
    me_u, me_c = me_s // 2, lax.rem(me_s, 2)

    loads = [
        pltpu.make_async_copy(src, dst, lsem.at[n])
        for n, (src, dst) in enumerate(((sav, savv), (tw, twv), (lat, latv), (sw, swv)))
    ]
    for copy in loads:
        copy.start()
    my_cols = pl.ds(pl.multiple_of(me_t * Cl, Cl), Cl)
    mine = [
        pltpu.make_async_copy(og.at[pl.ds(f * Pl, Pl)], opad.at[pl.ds((f + 1) * Pl, Pl), my_cols], osem.at[f])
        for f in range(F)
    ]
    for copy in mine:
        copy.start()

    barrier = pltpu.get_barrier_semaphore()
    count = 0
    for ds_ in range(S):
        for dt in range(T):
            if ds_ == 0 and dt == 0:
                continue
            count += 1
            pl.semaphore_signal(
                barrier, inc=1, device_id=(me_z, lax.rem(me_s + ds_, S), lax.rem(me_t + dt, T)),
                device_id_type=MESH,
            )
    for dz in range(1, Z):
        count += 1
        pl.semaphore_signal(
            barrier, inc=1, device_id=(lax.rem(me_z + dz, Z), me_s, me_t), device_id_type=MESH
        )
    pl.semaphore_wait(barrier, count)

    ocopies = []
    for d in range(F):
        f = lax.rem(me_s + d, F)
        for dt in range(1, T):
            copy = pltpu.make_async_remote_copy(
                src_ref=og.at[pl.ds(pl.multiple_of(f * Pl, Pl), Pl)],
                dst_ref=opad.at[pl.ds(pl.multiple_of((f + 1) * Pl, Pl), Pl), my_cols],
                send_sem=osend.at[d, dt - 1], recv_sem=orecv.at[d, dt - 1],
                device_id=(me_z, me_s, lax.rem(me_t + dt, T)), device_id_type=MESH,
            )
            copy.start()
            ocopies.append(copy)

    opad[pl.ds(0, Pl), :] = jnp.zeros((Pl, C), BF16)
    opad[pl.ds((F + 1) * Pl, Pl), :] = jnp.zeros((Pl, C), BF16)
    hwide[pl.ds(0, 8), :] = jnp.zeros((8, C), F32)
    hwide[pl.ds(8 + HW, 8), :] = jnp.zeros((8, C), F32)
    for b in range(3):
        hs[b, pl.ds(0, WS), :] = jnp.zeros((WS, C), BF16)
        hs[b, pl.ds(WS + HW, WS), :] = jnp.zeros((WS, C), BF16)
    loads[0].wait()
    savt[...] = savv[...].T
    loads[2].wait()
    latt[...] = latv[...].T
    loads[1].wait()
    loads[3].wait()
    for copy in mine:
        copy.wait()
    for copy in ocopies:
        copy.wait()

    hcopies = []
    for d in list(range(1, S)) + [0]:
        f = lax.rem(me_s + d, S)
        rows = pl.ds(pl.multiple_of(f * Pl, Pl), Pl)
        total = None
        for k in range(KT):
            moved = opad[pl.ds(pl.multiple_of((f + KT - 1 - k) * Pl, Pl), Pl), :]
            term = nt(moved, twv[k])
            total = term if total is None else total + term
        hsend[rows, :] = total.astype(BF16)
        dst = hrecv.at[pl.ds(pl.multiple_of(me_s * Pl, Pl), Pl), my_cols]
        for dt in range(T):
            if d == 0 and dt == 0:
                own = pltpu.make_async_copy(hsend.at[rows], dst, hlocsem)
                own.start()
                continue
            copy = pltpu.make_async_remote_copy(
                src_ref=hsend.at[rows], dst_ref=dst,
                send_sem=hsendsem.at[d, dt], recv_sem=hrecvsem.at[d, dt],
                device_id=(me_z, f, lax.rem(me_t + dt, T)), device_id_type=MESH,
            )
            copy.start()
            hcopies.append(copy)

    sent = {}

    def store_partial(tap, part):
        for s in range(S):
            gsend[s % 2, s // 2, tap] = part[:, s * Cs : (s + 1) * Cs].astype(BF16)

    def start1(n):
        at, size = chunks[n]
        copy = pltpu.make_async_remote_copy(
            src_ref=gsend.at[1 - me_c, :, pl.ds(at, size)], dst_ref=g1.at[:, pl.ds(at, size)],
            send_sem=s1s.at[n], recv_sem=s1r.at[n],
            device_id=(me_z, me_u * 2 + 1 - me_c, me_t), device_id_type=MESH,
        )
        copy.start()
        sent[1, n] = [copy]

    def step1(n):
        at, size = chunks[n]
        taps = pl.ds(at, size)
        for copy in sent[1, n]:
            copy.wait()
        g2s[:, taps] = (gsend[me_c, :, taps].astype(F32) + g1[:, taps].astype(F32)).astype(BF16)
        copies = []
        for d in range(1, U):
            other = lax.rem(me_u + d, U)
            copy = pltpu.make_async_remote_copy(
                src_ref=g2s.at[other, taps], dst_ref=g2r.at[d - 1, taps],
                send_sem=s2s.at[n, d - 1], recv_sem=s2r.at[n, d - 1],
                device_id=(me_z, other * 2 + me_c, me_t), device_id_type=MESH,
            )
            copy.start()
            copies.append(copy)
        sent[2, n] = copies

    def step2(n):
        at, size = chunks[n]
        taps = pl.ds(at, size)
        for copy in sent[2, n]:
            copy.wait()
        total = g2s[me_u, taps].astype(F32)
        for d in range(1, U):
            total = total + g2r[d - 1, taps].astype(F32)
        gz[taps] = total.astype(BF16)
        copies = []
        for d in range(1, Z):
            other = lax.rem(me_z + d, Z)
            copy = pltpu.make_async_remote_copy(
                src_ref=gz.at[taps, pl.ds(pl.multiple_of(other * Q, Q), Q)],
                dst_ref=g3r.at[d - 1, taps],
                send_sem=s3s.at[n, d - 1], recv_sem=s3r.at[n, d - 1],
                device_id=(other, me_s, me_t), device_id_type=MESH,
            )
            copy.start()
            copies.append(copy)
        sent[3, n] = copies

    def step3(n):
        at, size = chunks[n]
        taps = pl.ds(at, size)
        rows = pl.ds(pl.multiple_of(me_z * Q, Q), Q)
        for copy in sent[3, n]:
            copy.wait()
        total = gz[taps, rows].astype(F32)
        for d in range(1, Z):
            total = total + g3r[d - 1, taps].astype(F32)
        total = total.astype(BF16)
        gq[taps] = total
        gf[taps, rows] = total
        copies = []
        for d in range(1, Z):
            copy = pltpu.make_async_remote_copy(
                src_ref=gq.at[taps], dst_ref=gf.at[taps, rows],
                send_sem=s4s.at[n, d - 1], recv_sem=s4r.at[n, d - 1],
                device_id=(lax.rem(me_z + d, Z), me_s, me_t), device_id_type=MESH,
            )
            copy.start()
            copies.append(copy)
        sent[4, n] = copies

    def step4(n):
        at, size = chunks[n]
        for copy in sent[4, n]:
            copy.wait()
        value = gf[pl.ds(at, size)].astype(F32) * scale
        if at < KT:
            tg[pl.ds(at, size)] = value
        else:
            sg[pl.ds(at - KT, size)] = value

    first = len([0 for at, _ in chunks if at < KT])
    for n in range(first):
        at, size = chunks[n]

        @pl.loop(at, at + size)
        def _(k):
            moved = opad[pl.ds(pl.multiple_of((KT - 1 - k) * Pl, Pl), F * Pl), :]
            store_partial(k, nn(savt[...], moved))

        start1(n)
    for n in range(first):
        step1(n)

    own.wait()
    for copy in hcopies:
        copy.wait()

    tile = 4 * WS
    for r in range(0, HW, tile):
        hwide[pl.ds(8 + r, tile), :] = hrecv[pl.ds(r, tile), :].astype(F32)
        hs[1, pl.ds(WS + r, tile), :] = hrecv[pl.ds(r, tile), :]
    column = lax.rem(lax.broadcasted_iota(jnp.int32, (tile, C), 0), WS)
    for b in (-1, 1):
        keep = column != (0 if b == 1 else WS - 1)
        for r in range(0, HW, tile):
            value = hwide[pl.ds(8 + r - b, tile), :]
            hs[b + 1, pl.ds(WS + r, tile), :] = jnp.where(keep, value, 0.0).astype(BF16)

    def moved_at(tap):
        row, col = tap // 3, lax.rem(tap, 3)
        return hs[col, pl.ds(pl.multiple_of((2 - row) * WS, WS), HW), :]

    def gradient(n):
        at, size = chunks[n]

        @pl.loop(at - KT, at - KT + size)
        def _(tap):
            store_partial(tap + KT, nn(latt[...], moved_at(tap)))

        start1(n)

    def image(lo, hi):
        @pl.loop(lo, hi)
        def _(tap):
            term = nt(moved_at(tap), swv[tap])
            if lo == 0:
                @pl.when(tap == 0)
                def _():
                    acc[...] = term

                @pl.when(tap > 0)
                def _():
                    acc[...] += term
            else:
                acc[...] += term

    total = len(chunks)
    work = [("g", n) for n in range(first, total)] + [("i", n) for n in range(3)]
    done = {n: 1 for n in range(first)}
    for kind, n in work:
        if kind == "g":
            gradient(n)
        else:
            image(3 * n, 3 * n + 3)
        for m in range(total):
            if m in done and done[m] < 4:
                done[m] += 1
                (None, step1, step2, step3, step4)[done[m]](m)
        if kind == "g":
            done[n] = 0
    ig[...] = acc[...].astype(BF16)
    while any(done[m] < 4 for m in done):
        for m in range(total):
            if done[m] < 4:
                done[m] += 1
                (None, step1, step2, step3, step4)[done[m]](m)


def fused(sizes, chunk, latents, saved_input, out_grad, temporal_weight, spatial_weight):
    S, T, Z = sizes
    F, Pl, Cl = out_grad.shape[1:]
    KT, _, C = temporal_weight.shape
    taps = KT + spatial_weight.shape[0]
    HW = latents.shape[2]
    Cs = C // S
    U, Q = S // 2, Cl // Z
    scale = 1.0 / math.sqrt(Z * F * HS * WS)
    chunks = chunks_of(KT, chunk) + [(KT + at, n) for at, n in chunks_of(taps - KT, chunk)]
    N = len(chunks)
    dims = (S, T, Z, F, Pl, Cl, Cs, scale, chunks, KT)
    V = pltpu.VMEM
    D = pltpu.SemaphoreType.DMA
    hbm = pl.BlockSpec(memory_space=pl.ANY)
    vmem = pl.BlockSpec(memory_space=pltpu.VMEM)
    ig, tg, sg = pl.pallas_call(
        functools.partial(kernel, dims),
        out_shape=(
            jax.ShapeDtypeStruct((HW, Cl), BF16),
            jax.ShapeDtypeStruct((KT, Cl, Cs), F32),
            jax.ShapeDtypeStruct((taps - KT, Cl, Cs), F32),
        ),
        in_specs=[hbm] * 5,
        out_specs=(vmem,) * 3,
        scratch_shapes=[
            V((HW, Cl), BF16), V((F * Pl, Cl), BF16), V((KT, Cl, C), BF16), V((taps - KT, Cl, C), BF16),
            V(((F + 2) * Pl, C), BF16), V((F * Pl, Cl), BF16), V((HW, C), BF16),
            V((HW + 16, C), F32), V((3, HW + 2 * WS, C), BF16),
            V((Cl, F * Pl), BF16), V((Cl, HW), BF16), V((HW, Cl), F32),
            V((2, U, taps, Cl, Cs), BF16), V((U, taps, Cl, Cs), BF16), V((U, taps, Cl, Cs), BF16),
            V((U - 1, taps, Cl, Cs), BF16), V((taps, Cl, Cs), BF16), V((Z - 1, taps, Q, Cs), BF16),
            V((taps, Q, Cs), BF16), V((taps, Cl, Cs), BF16),
            D((4,)), D((F, T - 1)), D((F, T - 1)), D((F,)), D((S, T)), D((S, T)), D(()),
            D((N,)), D((N,)), D((N, U - 1)), D((N, U - 1)),
            D((N, Z - 1)), D((N, Z - 1)), D((N, Z - 1)), D((N, Z - 1)),
        ],
        compiler_params=pltpu.CompilerParams(
            collective_id=0, has_side_effects=True, vmem_limit_bytes=60 * 2**20
        ),
    )(
        latents.reshape(HW, Cl), saved_input.reshape(F * Pl, Cl), out_grad.reshape(F * Pl, Cl),
        temporal_weight, spatial_weight,
    )
    return ig.reshape(latents.shape), tg, sg


def plain(latents, saved_input, out_grad, temporal_weight, spatial_weight):
    clips_all = latents.shape[0] * lax.axis_size("clip")
    frames_all = latents.shape[1] * lax.axis_size("sp")
    scale_factor = 1.0 / math.sqrt(clips_all * frames_all * HS * WS)
    frames_count = out_grad.shape[1]
    local_in = temporal_weight.shape[1]
    saved_padded = pad_frames(saved_input)
    block_in = lax.all_gather(out_grad, "tp", axis=3, tiled=True)
    padded = pad_frames(block_in)
    hidden_acc = jnp.zeros(out_grad.shape[:3] + (local_in,), F32)
    parts = []
    for tap_index in range(3):
        shifted = padded[:, 2 - tap_index : 2 - tap_index + frames_count]
        hidden_acc = hidden_acc + jnp.einsum(
            "bfpo,io->bfpi", shifted, temporal_weight[tap_index], preferred_element_type=F32
        )
        window = saved_padded[:, tap_index : tap_index + frames_count]
        parts.append(jnp.einsum("bfpi,bfpo->io", window, block_in, preferred_element_type=F32))
    temporal_local = jnp.stack(parts)
    hidden_grad = hidden_acc.astype(BF16)
    regrouped = lax.all_to_all(hidden_grad, "sp", split_axis=1, concat_axis=2, tiled=True)
    batch = latents.shape[0] * latents.shape[1]
    image_pad = jnp.pad(latents.reshape(batch, HS, WS, local_in), ((0, 0), (1, 1), (1, 1), (0, 0)))
    block_in = lax.all_gather(regrouped, "tp", axis=3, tiled=True)
    whole = block_in.reshape(batch, HS, WS, block_in.shape[3])
    grid = jnp.pad(whole, ((0, 0), (1, 1), (1, 1), (0, 0)))
    input_acc = jnp.zeros((batch, HS, WS, local_in), F32)
    parts = []
    for row in (-1, 0, 1):
        for col in (-1, 0, 1):
            tap_index = 3 * (row + 1) + (col + 1)
            moved = grid[:, 1 - row : 1 - row + HS, 1 - col : 1 - col + WS]
            input_acc = input_acc + jnp.einsum(
                "gabo,co->gabc", moved, spatial_weight[tap_index], preferred_element_type=F32
            )
            window = image_pad[:, 1 + row : 1 + row + HS, 1 + col : 1 + col + WS]
            parts.append(jnp.einsum("gabc,gabo->co", window, whole, preferred_element_type=F32))
    spatial_local = jnp.stack(parts)
    input_grad = input_acc.reshape(latents.shape).astype(BF16)
    temporal_grad, spatial_grad = lax.psum(
        tuple(
            lax.psum_scatter(value * scale_factor, "sp", scatter_dimension=2, tiled=True)
            for value in (temporal_local, spatial_local)
        ),
        "clip",
    )
    return input_grad, temporal_grad, spatial_grad


CHUNK = 3


def solution(mesh):
    sizes = (mesh.shape["sp"], mesh.shape["tp"], mesh.shape["clip"])

    def local(latents, saved_input, out_grad, temporal_weight, spatial_weight):
        S, T, Z = sizes
        cols = temporal_weight.shape[2] // S
        fits = (
            latents.shape[:2] == (1, 1) and S % 2 == 0 and S > 2 and T > 1 and Z > 1
            and cols % 128 == 0 and out_grad.shape[3] % (16 * Z) == 0 and out_grad.shape[3] % 128 == 0
        )
        args = (latents, saved_input, out_grad, temporal_weight, spatial_weight)
        return fused(sizes, CHUNK, *args) if fits else plain(*args)

    return jax.shard_map(
        local,
        mesh=mesh,
        in_specs=(
            P("clip", "sp", None, "tp"),
            P("clip", None, "sp", "tp"),
            P("clip", None, "sp", "tp"),
            P(None, "tp", None),
            P(None, "tp", None),
        ),
        out_specs=(P("clip", "sp", None, "tp"), P(None, "tp", "sp"), P(None, "tp", "sp")),
        check_vma=False,
    )
```

time: 232 us -> 83.6 us (0.36)
  waiting for transfers between devices: 178 us -> 0 us
  Pallas kernels: 0 us -> 78 us
  matrix products: 18.6 us -> 0 us
  between operations: 14 us -> 0.65 us
  blocking collectives: 11.9 us -> 0 us
  other arithmetic: 4.25 us -> 0 us
    pallas_call x0 -> x1, Pallas kernels: none -> 78 us  [fused(): pl.pallas_call(functools.partial(kernel, dims), out_shape=(jax.ShapeDtype...]
    reduce_scatter x2 -> x0, waiting for transfers between devices: 67.9 us -> none  [the longest x1 50.3 us: local(): lax.psum_scatter(spatial_scaled, 'sp', scatter_dimension=2, tiled=True)]
    psum x1 -> x0, waiting for transfers between devices: 66.3 us -> none  [local(): temporal_grad, spatial_grad = lax.psum((spread[0], spread[1]), 'clip')]
    all_gather x2 -> x0, waiting for transfers between devices: 43 us -> none  [the longest x1 25.6 us: local(): block_in = lax.all_gather(out_grad, 'tp', axis=3, tiled=True)]
    dot_general x24 -> x0, matrix products: 18.6 us -> none  [the longest x9 9.08 us: local(): jnp.einsum('gabo,co->gabc', moved, columns[tap_index], preferred_element_...]
    all_to_all x1 -> x0, blocking collectives: 11.9 us -> none  [local(): lax.all_to_all(hidden_grad, 'sp', split_axis=1, concat_axis=2, tiled=True)]
    mul x2 -> x0, other arithmetic: 4.25 us -> none  [the longest x1 2.91 us: local(): spatial_scaled = spatial_local * scale_factor]
    unnamed x15 -> x5, local copies, waits for them, and re-layouts: 4.51 us -> 4.75 us
  transfers between devices with their start and end apart: 5 -> 0, of which waited for: 5 -> 0; matrix products, arithmetic and copies ran while one was open for 9% -> 0% of each run, Pallas kernels for 0% -> 0%
where the time goes in v1:
time: 83.6 us; the launch traced here: 83.4 us
  Pallas kernels  78 us (93%)
  local copies, waits for them, and re-layouts  4.75 us (6%)
    pallas_call x1, Pallas kernels, fused(): pl.pallas_call(functools.partial(kernel, dims), out_shape=(jax.ShapeDtype...  78 us
    unnamed x5, local copies, waits for them, and re-layouts  4.75 us

profile of v1, /device:TPU:0, one launch (start us, length us, event | category | flops | bytes accessed | tf_op | source)
XLA Modules:
  0.0 83.4 jit_solution(1674386325774802692)
XLA Ops:
  0.6 78.0 %shard_map.76 = (bf16[1024,256]{1,0:T(8,128)(2,1)}, f32[3,256,128]{2,1,0:T(8,128)}, f32[9,256,128]{2,1,0:T(8,128)}) custom-call(bf16[1024,256]{1,0:T(8,128)(2,1)} %bitcast.4, bf16[1024,256]{1,0:T(8,128)(2,1)} %bitcast.5, bf16[1024,256]{1,0:T(8,128)(2,1)} %bitcast.6, bf16[3,256,512]{2,1,0:T(8,128)(2,1)} %tw.1, bf16[9,256,512]{2,1,0:T(8,128)(2,1)} %sw.1), custom_call_target="tpu_custom_call" | custom-call | tf_op jit(solution)/shard_map/pallas_call | solution.py:319
  78.7 0.0 copy-start
  78.7 2.0 %copy.11 = bf16[1,1,1024,256]{3,2,1,0:T(8,128)(2,1)} copy(bf16[1,1,1024,256]{3,2,1,0:T(8,128)(2,1)} %bitcast.7) | data formatting | bytes 1048576
  80.6 1.8 %copy.12 = f32[3,256,128]{2,1,0:T(8,128)} copy(f32[3,256,128]{2,1,0:T(8,128)} %get-tuple-element.13) | data formatting | bytes 786432
  82.4 0.0 copy-done
  82.4 1.0 %copy.13 = f32[9,256,128]{2,1,0:T(8,128)} copy(f32[9,256,128]{2,1,0:T(8,128)S(1)} %copy-done) | data formatting | bytes 2359296
Async XLA Ops:
  78.7 3.7 %copy-start = (f32[9,256,128]{2,1,0:T(8,128)S(1)}, f32[9,256,128]{2,1,0:T(8,128)}, u32[]{:S(2)}) copy-start(f32[9,256,128]{2,1,0:T(8,128)} %get-tuple-element.14) | copy-start | bytes 3538948

commit v2 on v1

--- a/solution.py
+++ b/solution.py
@@ -31,16 +31,55 @@
     return [(start, min(size, taps - start)) for start in range(0, taps, size)]
 
 
+def order(chunks, first, images, tap_kb):
+    hop, rate = 2.0, 45.0 / 1.0
+    now, free = 0.0, {"core": 0.0, "x": 0.0, "z": 0.0, "back": 0.0}
+    pending, out = {}, []
+
+    def send(link, n, step):
+        cost = chunks[n][1] * tap_kb / rate if link != "core" else chunks[n][1] * tap_kb / 100.0
+        free[link] = max(free[link], now) + cost
+        pending[step, n] = free[link] + hop
+
+    for n in range(first):
+        send("x", n, 2)
+    grads, filler = list(range(first, len(chunks))), list(range(images))
+    while pending or grads or filler:
+        ready = sorted((at, key) for key, at in pending.items() if at <= now)
+        if grads and (not ready or len(ready) < 2):
+            n = grads.pop(0)
+            out.append(("g", n))
+            now += 0.6 * chunks[n][1]
+            send("core", n, 1)
+        elif ready or not filler:
+            at, (step, n) = ready[0] if ready else min((at, key) for key, at in pending.items())
+            now = max(now, at) + 0.12 * chunks[n][1]
+            del pending[step, n]
+            out.append((step, n))
+            if step == 1:
+                send("x", n, 2)
+            elif step == 2:
+                send("z", n, 3)
+            elif step == 3:
+                send("z", n, 4)
+            elif step == 4:
+                send("back", n, 5)
+        else:
+            n = filler.pop(0)
+            out.append(("i", n))
+            now += 0.7
+    return out
+
+
 def kernel(
     dims, lat, sav, og, tw, sw, ig, tg, sg,
     latv, savv, twv, swv, opad, hsend, hrecv, hwide, hs, savt, latt, acc,
-    gsend, g1, g2s, g2r, gz, g3r, gq, gf,
+    gsend, g1, g2s, g2r, gz, gzr, gf,
     lsem, osend, orecv, osem, hsendsem, hrecvsem, hlocsem,
-    s1s, s1r, s2s, s2r, s3s, s3r, s4s, s4r,
+    s1s, s1r, s2s, s2r, s3s, s3r,
 ):
     S, T, Z, F, Pl, Cl, Cs, scale, chunks, KT = dims
     U = S // 2
-    Q = Cl // Z
     HW = S * Pl
     C = T * Cl
     me_s, me_t, me_z = lax.axis_index("sp"), lax.axis_index("tp"), lax.axis_index("clip")
@@ -81,6 +120,7 @@
     ocopies = []
     for d in range(F):
         f = lax.rem(me_s + d, F)
+        ocopies.append([])
         for dt in range(1, T):
             copy = pltpu.make_async_remote_copy(
                 src_ref=og.at[pl.ds(pl.multiple_of(f * Pl, Pl), Pl)],
@@ -89,7 +129,7 @@
                 device_id=(me_z, me_s, lax.rem(me_t + dt, T)), device_id_type=MESH,
             )
             copy.start()
-            ocopies.append(copy)
+            ocopies[-1].append(copy)
 
     opad[pl.ds(0, Pl), :] = jnp.zeros((Pl, C), BF16)
     opad[pl.ds((F + 1) * Pl, Pl), :] = jnp.zeros((Pl, C), BF16)
@@ -106,13 +146,17 @@
     loads[3].wait()
     for copy in mine:
         copy.wait()
-    for copy in ocopies:
-        copy.wait()
+    arrived = set()
 
     hcopies = []
     for d in list(range(1, S)) + [0]:
         f = lax.rem(me_s + d, S)
         rows = pl.ds(pl.multiple_of(f * Pl, Pl), Pl)
+        for need in range(d - 1, d + 2):
+            if need % F not in arrived:
+                arrived.add(need % F)
+                for copy in ocopies[need % F]:
+                    copy.wait()
         total = None
         for k in range(KT):
             moved = opad[pl.ds(pl.multiple_of((f + KT - 1 - k) * Pl, Pl), Pl), :]
@@ -176,52 +220,99 @@
         for d in range(1, U):
             total = total + g2r[d - 1, taps].astype(F32)
         gz[taps] = total.astype(BF16)
-        copies = []
-        for d in range(1, Z):
-            other = lax.rem(me_z + d, Z)
-            copy = pltpu.make_async_remote_copy(
-                src_ref=gz.at[taps, pl.ds(pl.multiple_of(other * Q, Q), Q)],
-                dst_ref=g3r.at[d - 1, taps],
-                send_sem=s3s.at[n, d - 1], recv_sem=s3r.at[n, d - 1],
-                device_id=(other, me_s, me_t), device_id_type=MESH,
-            )
-            copy.start()
-            copies.append(copy)
-        sent[3, n] = copies
+
+        @pl.when(jnp.logical_and(is_end, jnp.logical_not(is_inner)))
+        def _():
+            to_inner(n).start()
+
+    half = Z // 2
+    low = me_z < half
+    is_end = jnp.logical_or(me_z == 0, me_z == Z - 1)
+    is_inner = jnp.logical_or(me_z == half - 1, me_z == half)
+    z_in = jnp.where(low, me_z + 1, me_z - 1)
+    z_out = jnp.clip(jnp.where(low, me_z - 1, me_z + 1), 0, Z - 1)
+    Z_INNER, Z_OUTER = 0, 1
+
+    def hop(n, src, slot, target):
+        at, size = chunks[n]
+        taps = pl.ds(at, size)
+        return pltpu.make_async_remote_copy(
+            src_ref=src.at[taps], dst_ref=gzr.at[slot, taps],
+            send_sem=s3s.at[slot, n], recv_sem=s3r.at[slot, n],
+            device_id=(target, me_s, me_t), device_id_type=MESH,
+        )
+
+    def to_inner(n):
+        return hop(n, gz, Z_OUTER, z_in)
+
+    def across(n):
+        return hop(n, gz, Z_INNER, z_in)
+
+    def to_outer(n):
+        return hop(n, gf, Z_INNER, z_out)
 
     def step3(n):
         at, size = chunks[n]
         taps = pl.ds(at, size)
-        rows = pl.ds(pl.multiple_of(me_z * Q, Q), Q)
-        for copy in sent[3, n]:
-            copy.wait()
-        total = gz[taps, rows].astype(F32)
-        for d in range(1, Z):
-            total = total + g3r[d - 1, taps].astype(F32)
-        total = total.astype(BF16)
-        gq[taps] = total
-        gf[taps, rows] = total
-        copies = []
-        for d in range(1, Z):
-            copy = pltpu.make_async_remote_copy(
-                src_ref=gq.at[taps], dst_ref=gf.at[taps, rows],
-                send_sem=s4s.at[n, d - 1], recv_sem=s4r.at[n, d - 1],
-                device_id=(lax.rem(me_z + d, Z), me_s, me_t), device_id_type=MESH,
-            )
-            copy.start()
-            copies.append(copy)
-        sent[4, n] = copies
-
-    def step4(n):
-        at, size = chunks[n]
-        for copy in sent[4, n]:
-            copy.wait()
+
+        @pl.when(jnp.logical_not(is_end))
+        def _():
+            to_inner(n).wait_recv()
+            gz[taps] = (gz[taps].astype(F32) + gzr[Z_OUTER, taps].astype(F32)).astype(BF16)
+
+            @pl.when(jnp.logical_not(is_inner))
+            def _():
+                to_inner(n).start()
+
+        @pl.when(is_inner)
+        def _():
+            across(n).start()
+
+    def output(n):
+        at, size = chunks[n]
         value = gf[pl.ds(at, size)].astype(F32) * scale
         if at < KT:
             tg[pl.ds(at, size)] = value
         else:
             sg[pl.ds(at - KT, size)] = value
 
+        @pl.when(jnp.logical_not(is_end))
+        def _():
+            to_outer(n).start()
+
+    def step4(n):
+        at, size = chunks[n]
+        taps = pl.ds(at, size)
+
+        @pl.when(is_inner)
+        def _():
+            across(n).wait_recv()
+            gf[taps] = (gz[taps].astype(F32) + gzr[Z_INNER, taps].astype(F32)).astype(BF16)
+            output(n)
+
+    def step5(n):
+        at, size = chunks[n]
+        taps = pl.ds(at, size)
+
+        @pl.when(jnp.logical_not(is_inner))
+        def _():
+            across(n).wait_recv()
+            gf[taps] = gzr[Z_INNER, taps]
+            output(n)
+
+    def finish(n):
+        @pl.when(is_inner)
+        def _():
+            across(n).wait_send()
+
+        @pl.when(jnp.logical_not(is_inner))
+        def _():
+            to_inner(n).wait_send()
+
+        @pl.when(jnp.logical_not(is_end))
+        def _():
+            to_outer(n).wait_send()
+
     first = len([0 for at, _ in chunks if at < KT])
     for n in range(first):
         at, size = chunks[n]
@@ -232,12 +323,12 @@
             store_partial(k, nn(savt[...], moved))
 
         start1(n)
-    for n in range(first):
-        step1(n)
-
     own.wait()
     for copy in hcopies:
         copy.wait()
+
+    for n in range(first):
+        step1(n)
 
     tile = 4 * WS
     for r in range(0, HW, tile):
@@ -263,41 +354,28 @@
 
         start1(n)
 
-    def image(lo, hi):
-        @pl.loop(lo, hi)
-        def _(tap):
-            term = nt(moved_at(tap), swv[tap])
-            if lo == 0:
-                @pl.when(tap == 0)
-                def _():
-                    acc[...] = term
-
-                @pl.when(tap > 0)
-                def _():
-                    acc[...] += term
-            else:
-                acc[...] += term
-
+    taps_left = swv.shape[0]
+
+    def image(tap):
+        term = nt(moved_at(tap), swv[tap])
+        if tap == 0:
+            acc[...] = term
+        elif tap < taps_left - 1:
+            acc[...] += term
+        else:
+            ig[...] = (acc[...] + term).astype(BF16)
+
+    steps = {1: step1, 2: step2, 3: step3, 4: step4, 5: step5}
     total = len(chunks)
-    work = [("g", n) for n in range(first, total)] + [("i", n) for n in range(3)]
-    done = {n: 1 for n in range(first)}
-    for kind, n in work:
+    for kind, n in order(chunks, first, taps_left, Cl * Cs * 2e-3):
         if kind == "g":
             gradient(n)
+        elif kind == "i":
+            image(n)
         else:
-            image(3 * n, 3 * n + 3)
-        for m in range(total):
-            if m in done and done[m] < 4:
-                done[m] += 1
-                (None, step1, step2, step3, step4)[done[m]](m)
-        if kind == "g":
-            done[n] = 0
-    ig[...] = acc[...].astype(BF16)
-    while any(done[m] < 4 for m in done):
-        for m in range(total):
-            if done[m] < 4:
-                done[m] += 1
-                (None, step1, step2, step3, step4)[done[m]](m)
+            steps[kind](n)
+    for n in range(total):
+        finish(n)
 
 
 def fused(sizes, chunk, latents, saved_input, out_grad, temporal_weight, spatial_weight):
@@ -307,7 +385,7 @@
     taps = KT + spatial_weight.shape[0]
     HW = latents.shape[2]
     Cs = C // S
-    U, Q = S // 2, Cl // Z
+    U = S // 2
     scale = 1.0 / math.sqrt(Z * F * HS * WS)
     chunks = chunks_of(KT, chunk) + [(KT + at, n) for at, n in chunks_of(taps - KT, chunk)]
     N = len(chunks)
@@ -331,11 +409,11 @@
             V((HW + 16, C), F32), V((3, HW + 2 * WS, C), BF16),
             V((Cl, F * Pl), BF16), V((Cl, HW), BF16), V((HW, Cl), F32),
             V((2, U, taps, Cl, Cs), BF16), V((U, taps, Cl, Cs), BF16), V((U, taps, Cl, Cs), BF16),
-            V((U - 1, taps, Cl, Cs), BF16), V((taps, Cl, Cs), BF16), V((Z - 1, taps, Q, Cs), BF16),
-            V((taps, Q, Cs), BF16), V((taps, Cl, Cs), BF16),
+            V((U - 1, taps, Cl, Cs), BF16), V((taps, Cl, Cs), BF16), V((2, taps, Cl, Cs), BF16),
+            V((taps, Cl, Cs), BF16),
             D((4,)), D((F, T - 1)), D((F, T - 1)), D((F,)), D((S, T)), D((S, T)), D(()),
             D((N,)), D((N,)), D((N, U - 1)), D((N, U - 1)),
-            D((N, Z - 1)), D((N, Z - 1)), D((N, Z - 1)), D((N, Z - 1)),
+            D((2, N)), D((2, N)),
         ],
         compiler_params=pltpu.CompilerParams(
             collective_id=0, has_side_effects=True, vmem_limit_bytes=60 * 2**20
@@ -396,7 +474,7 @@
     return input_grad, temporal_grad, spatial_grad
 
 
-CHUNK = 3
+CHUNK = 1
 
 
 def solution(mesh):
@@ -406,8 +484,8 @@
         S, T, Z = sizes
         cols = temporal_weight.shape[2] // S
         fits = (
-            latents.shape[:2] == (1, 1) and S % 2 == 0 and S > 2 and T > 1 and Z > 1
-            and cols % 128 == 0 and out_grad.shape[3] % (16 * Z) == 0 and out_grad.shape[3] % 128 == 0
+            latents.shape[:2] == (1, 1) and S % 2 == 0 and S > 2 and T > 1 and Z % 2 == 0
+            and cols % 128 == 0 and out_grad.shape[3] % 128 == 0
         )
         args = (latents, saved_input, out_grad, temporal_weight, spatial_weight)
         return fused(sizes, CHUNK, *args) if fits else plain(*args)

time: 83.6 us -> 72.5 us (0.87)
  Pallas kernels: 78 us -> 66.9 us
    pallas_call x1, Pallas kernels: 78 us -> 66.9 us  [fused(): pl.pallas_call(functools.partial(kernel, dims), out_shape=(jax.ShapeDtype...]
where the time goes in v2:
time: 72.5 us; the launch traced here: 72.3 us
  Pallas kernels  66.9 us (92%)
  local copies, waits for them, and re-layouts  4.75 us (7%)
    pallas_call x1, Pallas kernels, fused(): pl.pallas_call(functools.partial(kernel, dims), out_shape=(jax.ShapeDtype...  66.9 us
    unnamed x5, local copies, waits for them, and re-layouts  4.75 us

profile of v2, /device:TPU:0, one launch (start us, length us, event | category | flops | bytes accessed | tf_op | source)
XLA Modules:
  0.0 72.3 jit_solution(14086368929830144185)
XLA Ops:
  0.6 66.9 %shard_map.76 = (bf16[1024,256]{1,0:T(8,128)(2,1)}, f32[3,256,128]{2,1,0:T(8,128)}, f32[9,256,128]{2,1,0:T(8,128)}) custom-call(bf16[1024,256]{1,0:T(8,128)(2,1)} %bitcast.4, bf16[1024,256]{1,0:T(8,128)(2,1)} %bitcast.5, bf16[1024,256]{1,0:T(8,128)(2,1)} %bitcast.6, bf16[3,256,512]{2,1,0:T(8,128)(2,1)} %tw.1, bf16[9,256,512]{2,1,0:T(8,128)(2,1)} %sw.1), custom_call_target="tpu_custom_call" | custom-call | tf_op jit(solution)/shard_map/pallas_call | solution.py:397
  67.6 0.0 copy-start
  67.6 2.0 %copy.11 = bf16[1,1,1024,256]{3,2,1,0:T(8,128)(2,1)} copy(bf16[1,1,1024,256]{3,2,1,0:T(8,128)(2,1)} %bitcast.7) | data formatting | bytes 1048576
  69.6 1.8 %copy.12 = f32[3,256,128]{2,1,0:T(8,128)} copy(f32[3,256,128]{2,1,0:T(8,128)} %get-tuple-element.13) | data formatting | bytes 786432
  71.3 0.0 copy-done
  71.3 1.0 %copy.13 = f32[9,256,128]{2,1,0:T(8,128)} copy(f32[9,256,128]{2,1,0:T(8,128)S(1)} %copy-done) | data formatting | bytes 2359296
Async XLA Ops:
  67.6 3.7 %copy-start = (f32[9,256,128]{2,1,0:T(8,128)S(1)}, f32[9,256,128]{2,1,0:T(8,128)}, u32[]{:S(2)}) copy-start(f32[9,256,128]{2,1,0:T(8,128)} %get-tuple-element.14) | copy-start | bytes 3538948

commit v3 on v2

--- a/solution.py
+++ b/solution.py
@@ -32,7 +32,7 @@
 
 
 def order(chunks, first, images, tap_kb):
-    hop, rate = 2.0, 45.0 / 1.0
+    hop, rate = 2.5, 40.0
     now, free = 0.0, {"core": 0.0, "x": 0.0, "z": 0.0, "back": 0.0}
     pending, out = {}, []
 
@@ -49,7 +49,7 @@
         if grads and (not ready or len(ready) < 2):
             n = grads.pop(0)
             out.append(("g", n))
-            now += 0.6 * chunks[n][1]
+            now += 0.8 * chunks[n][1]
             send("core", n, 1)
         elif ready or not filler:
             at, (step, n) = ready[0] if ready else min((at, key) for key, at in pending.items())
@@ -72,9 +72,9 @@
 
 
 def kernel(
-    dims, lat, sav, og, tw, sw, ig, tg, sg,
+    dims, lat, sav, og, tw, sw, ig, gf,
     latv, savv, twv, swv, opad, hsend, hrecv, hwide, hs, savt, latt, acc,
-    gsend, g1, g2s, g2r, gz, gzr, gf,
+    gsend, g1, g2s, g2r, gz, gzf, gzr,
     lsem, osend, orecv, osem, hsendsem, hrecvsem, hlocsem,
     s1s, s1r, s2s, s2r, s3s, s3r,
 ):
@@ -216,9 +216,10 @@
         taps = pl.ds(at, size)
         for copy in sent[2, n]:
             copy.wait()
-        total = g2s[me_u, taps].astype(F32)
+        total = gsend[me_c, me_u, taps].astype(F32) + g1[me_u, taps].astype(F32)
         for d in range(1, U):
             total = total + g2r[d - 1, taps].astype(F32)
+        gzf[taps] = total
         gz[taps] = total.astype(BF16)
 
         @pl.when(jnp.logical_and(is_end, jnp.logical_not(is_inner)))
@@ -258,7 +259,7 @@
         @pl.when(jnp.logical_not(is_end))
         def _():
             to_inner(n).wait_recv()
-            gz[taps] = (gz[taps].astype(F32) + gzr[Z_OUTER, taps].astype(F32)).astype(BF16)
+            gz[taps] = (gzf[taps] + gzr[Z_OUTER, taps].astype(F32)).astype(BF16)
 
             @pl.when(jnp.logical_not(is_inner))
             def _():
@@ -269,13 +270,6 @@
             across(n).start()
 
     def output(n):
-        at, size = chunks[n]
-        value = gf[pl.ds(at, size)].astype(F32) * scale
-        if at < KT:
-            tg[pl.ds(at, size)] = value
-        else:
-            sg[pl.ds(at - KT, size)] = value
-
         @pl.when(jnp.logical_not(is_end))
         def _():
             to_outer(n).start()
@@ -323,12 +317,12 @@
             store_partial(k, nn(savt[...], moved))
 
         start1(n)
+    for n in range(first):
+        step1(n)
+
     own.wait()
     for copy in hcopies:
         copy.wait()
-
-    for n in range(first):
-        step1(n)
 
     tile = 4 * WS
     for r in range(0, HW, tile):
@@ -392,36 +386,51 @@
     dims = (S, T, Z, F, Pl, Cl, Cs, scale, chunks, KT)
     V = pltpu.VMEM
     D = pltpu.SemaphoreType.DMA
-    hbm = pl.BlockSpec(memory_space=pl.ANY)
+    hbm = pl.BlockSpec(memory_space=pltpu.HBM)
     vmem = pl.BlockSpec(memory_space=pltpu.VMEM)
-    ig, tg, sg = pl.pallas_call(
+    ig, sums = pl.pallas_call(
         functools.partial(kernel, dims),
         out_shape=(
             jax.ShapeDtypeStruct((HW, Cl), BF16),
-            jax.ShapeDtypeStruct((KT, Cl, Cs), F32),
-            jax.ShapeDtypeStruct((taps - KT, Cl, Cs), F32),
+            jax.ShapeDtypeStruct((taps, Cl, Cs), BF16),
         ),
         in_specs=[hbm] * 5,
-        out_specs=(vmem,) * 3,
+        out_specs=(vmem,) * 2,
         scratch_shapes=[
             V((HW, Cl), BF16), V((F * Pl, Cl), BF16), V((KT, Cl, C), BF16), V((taps - KT, Cl, C), BF16),
             V(((F + 2) * Pl, C), BF16), V((F * Pl, Cl), BF16), V((HW, C), BF16),
             V((HW + 16, C), F32), V((3, HW + 2 * WS, C), BF16),
             V((Cl, F * Pl), BF16), V((Cl, HW), BF16), V((HW, Cl), F32),
             V((2, U, taps, Cl, Cs), BF16), V((U, taps, Cl, Cs), BF16), V((U, taps, Cl, Cs), BF16),
-            V((U - 1, taps, Cl, Cs), BF16), V((taps, Cl, Cs), BF16), V((2, taps, Cl, Cs), BF16),
-            V((taps, Cl, Cs), BF16),
+            V((U - 1, taps, Cl, Cs), BF16), V((taps, Cl, Cs), BF16), V((taps, Cl, Cs), F32), V((2, taps, Cl, Cs), BF16),
             D((4,)), D((F, T - 1)), D((F, T - 1)), D((F,)), D((S, T)), D((S, T)), D(()),
             D((N,)), D((N,)), D((N, U - 1)), D((N, U - 1)),
             D((2, N)), D((2, N)),
         ],
         compiler_params=pltpu.CompilerParams(
-            collective_id=0, has_side_effects=True, vmem_limit_bytes=60 * 2**20
+            collective_id=0, has_side_effects=True, vmem_limit_bytes=63 * 2**20
         ),
     )(
         latents.reshape(HW, Cl), saved_input.reshape(F * Pl, Cl), out_grad.reshape(F * Pl, Cl),
         temporal_weight, spatial_weight,
     )
+
+    def finish(ig_ref, sums_ref, ig_out, tg_out, sg_out):
+        ig_out[...] = ig_ref[...]
+        tg_out[...] = sums_ref[:KT].astype(F32) * scale
+        sg_out[...] = sums_ref[KT:].astype(F32) * scale
+
+    ig, tg, sg = pl.pallas_call(
+        finish,
+        out_shape=(
+            jax.ShapeDtypeStruct((HW, Cl), BF16),
+            jax.ShapeDtypeStruct((KT, Cl, Cs), F32),
+            jax.ShapeDtypeStruct((taps - KT, Cl, Cs), F32),
+        ),
+        in_specs=[vmem] * 2,
+        out_specs=(vmem,) * 3,
+        compiler_params=pltpu.CompilerParams(vmem_limit_bytes=16 * 2**20),
+    )(ig, sums)
     return ig.reshape(latents.shape), tg, sg
 
 

time: 72.5 us -> 70.1 us (0.967)
  local copies, waits for them, and re-layouts: 4.75 us -> 2.17 us
    unnamed x5 -> x4, local copies, waits for them, and re-layouts: 4.75 us -> 2.17 us
    pallas_call x0 -> x1, Pallas kernels: none -> 1.4 us  [fused(): pl.pallas_call(finish, out_shape=(jax.ShapeDtypeStruct((HW, Cl), BF16), j...]
    pallas_call x1, Pallas kernels: 66.9 us -> 65.7 us  [fused(): pl.pallas_call(functools.partial(kernel, dims), out_shape=(jax.ShapeDtype...]
where the time goes in v3:
time: 70.1 us; the launch traced here: 69.9 us
  Pallas kernels  67.1 us (96%)
  local copies, waits for them, and re-layouts  2.17 us (3%)
    pallas_call x1, Pallas kernels, fused(): pl.pallas_call(functools.partial(kernel, dims), out_shape=(jax.ShapeDtype...  65.7 us
    unnamed x4, local copies, waits for them, and re-layouts  2.17 us
    pallas_call x1, Pallas kernels, fused(): pl.pallas_call(finish, out_shape=(jax.ShapeDtypeStruct((HW, Cl), BF16), j...  1.4 us

profile of v3, /device:TPU:0, one launch (start us, length us, event | category | flops | bytes accessed | tf_op | source)
XLA Modules:
  0.0 69.9 jit_solution(3895049425623177597)
XLA Ops:
  0.6 65.7 %shard_map.76 = (bf16[1024,256]{1,0:T(8,128)(2,1)}, bf16[12,256,128]{2,1,0:T(8,128)(2,1)}) custom-call(bf16[1024,256]{1,0:T(8,128)(2,1)} %bitcast.4, bf16[1024,256]{1,0:T(8,128)(2,1)} %bitcast.5, bf16[1024,256]{1,0:T(8,128)(2,1)} %bitcast.6, bf16[3,256,512]{2,1,0:T(8,128)(2,1)} %tw.1, bf16[9,256,512]{2,1,0:T(8,128)(2,1)} %sw.1), custom_call_target="tpu_custom_call" | custom-call | tf_op jit(solution)/shard_map/pallas_call | solution.py:391
  66.3 0.0 copy-start
  66.3 1.1 %copy-done = bf16[12,256,128]{2,1,0:T(8,128)(2,1)S(1)} copy-done((bf16[12,256,128]{2,1,0:T(8,128)(2,1)S(1)}, bf16[12,256,128]{2,1,0:T(8,128)(2,1)}, u32[]{:S(2)}) %copy-start) | copy-done | bytes 786456
  67.5 0.0 copy-start.1
  67.5 1.0 %copy-done.1 = bf16[1024,256]{1,0:T(8,128)(2,1)S(1)} copy-done((bf16[1024,256]{1,0:T(8,128)(2,1)S(1)}, bf16[1024,256]{1,0:T(8,128)(2,1)}, u32[]{:S(2)}) %copy-start.1) | copy-done | bytes 524312
  68.5 1.4 %shard_map.77 = (bf16[1024,256]{1,0:T(8,128)(2,1)}, f32[3,256,128]{2,1,0:T(8,128)}, f32[9,256,128]{2,1,0:T(8,128)}) custom-call(bf16[1024,256]{1,0:T(8,128)(2,1)S(1)} %copy-done.1, bf16[12,256,128]{2,1,0:T(8,128)(2,1)S(1)} %copy-done), custom_call_target="tpu_custom_call" | custom-call | tf_op jit(solution)/shard_map/pallas_call | solution.py:423
Async XLA Ops:
  66.3 1.1 %copy-start = (bf16[12,256,128]{2,1,0:T(8,128)(2,1)S(1)}, bf16[12,256,128]{2,1,0:T(8,128)(2,1)}, u32[]{:S(2)}) copy-start(bf16[12,256,128]{2,1,0:T(8,128)(2,1)} %get-tuple-element.9.sums_ref) | copy-start | bytes 2359300
  67.5 1.0 %copy-start.1 = (bf16[1024,256]{1,0:T(8,128)(2,1)S(1)}, bf16[1024,256]{1,0:T(8,128)(2,1)}, u32[]{:S(2)}) copy-start(bf16[1024,256]{1,0:T(8,128)(2,1)} %get-tuple-element.8.ig_ref) | copy-start | bytes 1572868

commit v4 on v3

--- a/solution.py
+++ b/solution.py
@@ -42,7 +42,7 @@
         pending[step, n] = free[link] + hop
 
     for n in range(first):
-        send("x", n, 2)
+        send("z", n, 3)
     grads, filler = list(range(first, len(chunks))), list(range(images))
     while pending or grads or filler:
         ready = sorted((at, key) for key, at in pending.items() if at <= now)
@@ -319,6 +319,8 @@
         start1(n)
     for n in range(first):
         step1(n)
+    for n in range(first):
+        step2(n)
 
     own.wait()
     for copy in hcopies:

time: 70.1 us -> 68.7 us (0.980)
  Pallas kernels: 67.1 us -> 65.7 us
    pallas_call x1, Pallas kernels: 65.7 us -> 64.3 us  [fused(): pl.pallas_call(functools.partial(kernel, dims), out_shape=(jax.ShapeDtype...]
where the time goes in v4:
time: 68.7 us; the launch traced here: 68.5 us
  Pallas kernels  65.7 us (96%)
  local copies, waits for them, and re-layouts  2.17 us (3%)
    pallas_call x1, Pallas kernels, fused(): pl.pallas_call(functools.partial(kernel, dims), out_shape=(jax.ShapeDtype...  64.3 us
    unnamed x4, local copies, waits for them, and re-layouts  2.17 us
    pallas_call x1, Pallas kernels, fused(): pl.pallas_call(finish, out_shape=(jax.ShapeDtypeStruct((HW, Cl), BF16), j...  1.4 us

profile of v4, /device:TPU:0, one launch (start us, length us, event | category | flops | bytes accessed | tf_op | source)
XLA Modules:
  0.0 68.5 jit_solution(13062659758024847109)
XLA Ops:
  0.6 64.3 %shard_map.76 = (bf16[1024,256]{1,0:T(8,128)(2,1)}, bf16[12,256,128]{2,1,0:T(8,128)(2,1)}) custom-call(bf16[1024,256]{1,0:T(8,128)(2,1)} %bitcast.4, bf16[1024,256]{1,0:T(8,128)(2,1)} %bitcast.5, bf16[1024,256]{1,0:T(8,128)(2,1)} %bitcast.6, bf16[3,256,512]{2,1,0:T(8,128)(2,1)} %tw.1, bf16[9,256,512]{2,1,0:T(8,128)(2,1)} %sw.1), custom_call_target="tpu_custom_call" | custom-call | tf_op jit(solution)/shard_map/pallas_call | solution.py:393
  64.9 0.0 copy-start
  64.9 1.1 %copy-done = bf16[12,256,128]{2,1,0:T(8,128)(2,1)S(1)} copy-done((bf16[12,256,128]{2,1,0:T(8,128)(2,1)S(1)}, bf16[12,256,128]{2,1,0:T(8,128)(2,1)}, u32[]{:S(2)}) %copy-start) | copy-done | bytes 786456
  66.0 0.0 copy-start.1
  66.0 1.0 %copy-done.1 = bf16[1024,256]{1,0:T(8,128)(2,1)S(1)} copy-done((bf16[1024,256]{1,0:T(8,128)(2,1)S(1)}, bf16[1024,256]{1,0:T(8,128)(2,1)}, u32[]{:S(2)}) %copy-start.1) | copy-done | bytes 524312
  67.1 1.4 %shard_map.77 = (bf16[1024,256]{1,0:T(8,128)(2,1)}, f32[3,256,128]{2,1,0:T(8,128)}, f32[9,256,128]{2,1,0:T(8,128)}) custom-call(bf16[1024,256]{1,0:T(8,128)(2,1)S(1)} %copy-done.1, bf16[12,256,128]{2,1,0:T(8,128)(2,1)S(1)} %copy-done), custom_call_target="tpu_custom_call" | custom-call | tf_op jit(solution)/shard_map/pallas_call | solution.py:425
Async XLA Ops:
  64.9 1.1 %copy-start = (bf16[12,256,128]{2,1,0:T(8,128)(2,1)S(1)}, bf16[12,256,128]{2,1,0:T(8,128)(2,1)}, u32[]{:S(2)}) copy-start(bf16[12,256,128]{2,1,0:T(8,128)(2,1)} %get-tuple-element.9.sums_ref) | copy-start | bytes 2359300
  66.0 1.0 %copy-start.1 = (bf16[1024,256]{1,0:T(8,128)(2,1)S(1)}, bf16[1024,256]{1,0:T(8,128)(2,1)}, u32[]{:S(2)}) copy-start(bf16[1024,256]{1,0:T(8,128)(2,1)} %get-tuple-element.8.ig_ref) | copy-start | bytes 1572868
